TPU v7x, 32 devices: a whole 2x2x4 slice. The times are simulated.
32 devices in a mesh: pb: 8 (over z, y), ka: 4 (over x, core).
Axes of the slice: x: 2, y: 2, z: 4, core: 2. Of those that a mesh axis runs over, the one named last changes fastest.
Arguments:
- query_rows: bfloat16 [4096, 512], P(('pb', 'ka')), may hold values from -8 to 8
- key_rows: bfloat16 [4096, 128], P(('pb', 'ka')), may hold values from -3 to 3
- value_rows: bfloat16 [4096, 128], P(('pb', 'ka')), may hold values from -6 to 6
- outputs: bfloat16 [4096, 512], P(('pb', 'ka')), may hold values from -3 to 3
- out_grads: bfloat16 [4096, 512], P(('pb', 'ka')), may hold values from -6 to 6
- log_totals: float32 [4, 4096], P(None, ('pb', 'ka'))
- selected: int32 [32, 2], P(('pb', 'ka')), may hold values from 0 to 31, as said below
- counts: int32 [32], P(('pb', 'ka')), may hold values from 1 to 2, as said below
Outputs:
- query_grad: float32 [4096, 512], P(('pb', 'ka'))
- key_grad: float32 [4096, 128], P(('pb', 'ka'))
- value_grad: float32 [4096, 128], P(('pb', 'ka'))
Inputs may be any that keep to these rules, and one draw needn't show every extreme that they name: `selected`: slot 0 of row q is q itself; the first counts[q] entries of row q are distinct blocks no later than q; entries from slot counts[q] on are padding and are ignored. counts[q] is at most q + 1; the last query block's count is 2.
All inputs are finite; a program needn't handle non-finite values.
Results may differ from a plain program's by a relative error of at most 0.0029.
Values may be sent and summed in bfloat16 or wider, within the bound.
A program may use at most 64 MiB of HBM per device.

v0:
```python
import jax
import jax.numpy as jnp
from jax import lax
from jax.sharding import PartitionSpec as P

VERY_LOW = -1e30


def passed_along(value, axis, steps):
    count = lax.axis_size(axis)
    pairs = [(source, (source + steps) % count) for source in range(count)]
    return lax.ppermute(value, axis, pairs)


def head_sums(grad_rows, out_rows, head_width):
    row_total = grad_rows.shape[0]
    part_heads = grad_rows.shape[1] // head_width
    product = grad_rows.astype(jnp.float32) * out_rows.astype(jnp.float32)
    return jnp.sum(product.reshape(row_total, part_heads, head_width), axis=2).T


def shards(query_rows, key_rows, value_rows, outputs, out_grads, log_totals, selected, counts):
    ka_count = lax.axis_size("ka")
    ka_index = lax.axis_index("ka")
    pb_index = lax.axis_index("pb")
    block_count = selected.shape[0]
    slot_count = selected.shape[1]
    head_width = key_rows.shape[1]
    block_rows = query_rows.shape[0] // block_count
    score_scale = head_width ** (-0.5)
    key_pairs = jnp.concatenate([key_rows, value_rows], 1)
    column_keys = lax.all_gather(key_pairs, "pb", axis=0, tiled=True)
    peer_slots, peer_counts = (
        lax.all_gather(selected, "ka", axis=0, tiled=True),
        lax.all_gather(counts, "ka", axis=0, tiled=True),
    )
    key_grads = jnp.zeros((column_keys.shape[0], 2 * head_width), jnp.float32)
    row_offsets = jnp.arange(block_rows, dtype=jnp.int32)
    flat_owner = jnp.repeat(jnp.arange(block_count, dtype=jnp.int32), slot_count)
    flat_slot = jnp.tile(jnp.arange(slot_count, dtype=jnp.int32), block_count)
    flat_places = jnp.arange(block_count * slot_count, dtype=jnp.int32)

    def visit_block(row_stack, query_grad, stat_stack, anchor, key_grads):
        held_query = row_stack[0]
        held_grad = row_stack[1]
        total_rows = stat_stack[0]
        delta_rows = head_sums(row_stack[1], row_stack[2], head_width)
        part_heads = total_rows.shape[0]
        held_slots = lax.dynamic_slice_in_dim(
            peer_slots, anchor * block_count, block_count, 0
        ).reshape(-1)
        held_counts = jnp.repeat(
            lax.dynamic_slice_in_dim(peer_counts, anchor * block_count, block_count, 0), slot_count
        )
        first_block = (pb_index * ka_count + anchor) * block_count
        wanted = (flat_slot < held_counts) & (held_slots // block_count % ka_count == ka_index)
        position = jnp.cumsum(wanted.astype(jnp.int32)) - 1
        placed = wanted[:, None] & (position[:, None] == flat_places[None, :])
        packed_ids = jnp.sum(jnp.where(placed, held_slots[:, None], 0), axis=0)
        packed_owner = jnp.sum(jnp.where(placed, flat_owner[:, None], 0), axis=0)
        live_tiles = jnp.sum(wanted.astype(jnp.int32))

        def one_tile(tile_index, loop_state):
            query_grad, key_grads = loop_state
            key_block = packed_ids[tile_index]
            owner_block = packed_owner[tile_index]
            key_start = (
                key_block // (block_count * ka_count) * block_count + key_block % block_count
            ) * block_rows
            pair_tile = lax.dynamic_slice_in_dim(column_keys, key_start, block_rows, 0)
            key_tile = pair_tile[:, :head_width]
            value_tile = pair_tile[:, head_width:]
            query_tile = held_query.reshape(block_rows, part_heads, head_width)
            grad_tile = held_grad.reshape(block_rows, part_heads, head_width)
            scores = (
                jnp.einsum("rhd,cd->hrc", query_tile, key_tile, preferred_element_type=jnp.float32)
                * score_scale
            )
            query_pos = (first_block + owner_block) * block_rows + row_offsets
            key_pos = key_block * block_rows + row_offsets
            allowed = key_pos[None, :] <= query_pos[:, None]
            probs_full = jnp.exp(
                jnp.where(allowed[None], scores - total_rows[:, :, None], VERY_LOW)
            )
            prob_grads = jnp.einsum(
                "rhd,cd->hrc", grad_tile, value_tile, preferred_element_type=jnp.float32
            )
            score_grads = probs_full * (prob_grads - delta_rows[:, :, None])
            rounded_probs = probs_full.astype(jnp.bfloat16)
            rounded_grads = score_grads.astype(jnp.bfloat16)
            value_part = jnp.einsum(
                "hrc,rhd->cd", rounded_probs, grad_tile, preferred_element_type=jnp.float32
            )
            key_part = (
                jnp.einsum(
                    "hrc,rhd->cd", rounded_grads, query_tile, preferred_element_type=jnp.float32
                )
                * score_scale
            )
            query_part = (
                jnp.einsum(
                    "hrc,cd->rhd", rounded_grads, key_tile, preferred_element_type=jnp.float32
                )
                * score_scale
            )
            old_query = query_grad
            query_grad = old_query + query_part.reshape(block_rows, -1)
            old_keys = lax.dynamic_slice_in_dim(key_grads, key_start, block_rows, 0)
            key_grads = lax.dynamic_update_slice_in_dim(
                key_grads, old_keys + jnp.concatenate([key_part, value_part], 1), key_start, 0
            )
            return (query_grad, key_grads)

        return lax.fori_loop(0, live_tiles, one_tile, (query_grad, key_grads))

    query_part = query_rows
    grad_zero = jnp.zeros(query_part.shape, jnp.float32)
    row_stack = jnp.stack([query_part, out_grads, outputs])
    query_grad = grad_zero
    stat_stack = log_totals[None]

    def forward_hop(hop_index, loop_state):
        row_stack, query_grad, stat_stack, key_grads = loop_state
        anchor = (ka_index - hop_index) % ka_count
        query_grad, key_grads = visit_block(row_stack, query_grad, stat_stack, anchor, key_grads)
        row_stack = passed_along(row_stack, "ka", 1)
        query_grad, stat_stack = passed_along((query_grad, stat_stack), "ka", 1)
        return (row_stack, query_grad, stat_stack, key_grads)

    row_stack, query_grad, stat_stack, key_grads = lax.fori_loop(
        0, ka_count - 1, forward_hop, (row_stack, query_grad, stat_stack, key_grads)
    )
    query_grad, key_grads = visit_block(
        row_stack, query_grad, stat_stack, (ka_index + 1) % ka_count, key_grads
    )
    query_grad = passed_along(query_grad, "ka", 1)
    owned_grads = lax.psum_scatter(key_grads, "pb", scatter_dimension=0, tiled=True)
    return (query_grad, owned_grads[:, :head_width], owned_grads[:, head_width:])


def solution(mesh):
    return jax.shard_map(
        shards,
        mesh=mesh,
        in_specs=(
            P(("pb", "ka"), None),
            P(("pb", "ka"), None),
            P(("pb", "ka"), None),
            P(("pb", "ka"), None),
            P(("pb", "ka"), None),
            P(None, ("pb", "ka")),
            P(("pb", "ka"), None),
            P(("pb", "ka")),
        ),
        out_specs=(P(("pb", "ka"), None), P(("pb", "ka"), None), P(("pb", "ka"), None)),
        check_vma=False,
    )
```

profile of v0, /device:TPU:0, one launch (start us, length us, event | category | flops | bytes accessed | tf_op | source)
XLA Modules:
  0.0 183.4 jit_solution(7212830723820672716)
XLA Ops:
  8.5 0.7 dynamic-slice
  9.2 0.8 dynamic-update-slice
  10.0 6.4 %all-reduce = s32[4]{0:T(128)S(1)} all-reduce(s32[4]{0:T(128)S(1)} %dynamic-update-slice), channel_id=1, replica_groups=mesh['pb'=8,'ka'=4] {'ka'}, use_global_device_ids=true, to_apply=%add | all-reduce | flops 4 | bytes 32
  16.4 0.7 copy-done.5
  17.0 5.0 %all-gather = s32[4,1,2]{2,1,0:T(1,128)S(1)} all-gather(s32[1,1,2]{2,1,0:T(1,128)S(1)} %bitcast.222), channel_id=1, replica_groups=mesh['pb'=8,'ka'=4] {'ka'}, dimensions={0}, use_global_device_ids=true | all-gather | bytes 40 | tf_op jit(solution)/shard_map/all_gather | solution.py:34
  22.7 1.3 convert_reduce_fusion.1
  24.5 1.1 copy.63
  25.7 0.8 copy-done.2
  27.3 31.9 %all_gather.11 = bf16[1024,256]{1,0:T(8,128)(2,1)S(1)} all-gather(bf16[128,256]{1,0:T(8,128)(2,1)S(1)} %pad_maximum_fusion.1), channel_id=1, replica_groups=mesh['pb'=8,'ka'=4] {'pb'}, dimensions={0}, use_global_device_ids=true | all-gather | bytes 589824 | tf_op jit(solution)/shard_map/all_gather | solution.py:32
  60.0 40.6 %while.86 = (s32[]{:T(128)}, bf16[3,128,512]{1,2,0:T(8,128)(2,1)S(1)}, f32[128,512]{0,1:T(8,128)S(1)}, f32[1,4,128]{2,1,0:T(4,128)S(1)}, f32[1024,256]{0,1:T(8,1...) while((s32[]{:T(128)}, ...), condition=%wide.region_7.8_spmd.clone.clone, body=%wide.region_0.7_spmd.clone.clone.sunk | while | flops 84836216 | bytes 8673559 | solution.py:130
  60.1 0.7 dynamic_slice.117
  60.7 1.3 convert_reduce_fusion.3
  62.0 0.6 fusion.81
  63.1 6.2 %while.88 = (s32[]{:T(128)}, f32[128,512]{0,1:T(8,128)S(1)}, f32[1024,256]{0,1:T(8,128)S(1)}, s32[]{:T(128)}, s32[2]{0:T(128)S(1)}, /*index=5*/bf16[1024,256]{1,...) while((s32[]{:T(128)}, f32[128,512]{0,1:T(8,128)S(1)}, ...), condition=%wide.region_6.6_spmd.clone, body=%wide.region_5.5_spmd.clone.sunk | while | flops 84574488 | bytes 3415011 | solution.py:114
  69.3 1.0 collective-permute-start.1
  70.3 4.8 %collective-permute-done.1 = f32[128,512]{0,1:T(8,128)S(1)} collective-permute-done((f32[128,512]{0,1:T(8,128)S(1)}, f32[128,512]{0,1:T(8,128)S(1)}, u32[]{:S(2)}, u32[]{:S(2)}) %collective-permute-start.1) | collective-permute-done | bytes 262176 | tf_op jit(solution)/shard_map/while/body/eval_jaxpr/ppermute | solution.py:12
  75.3 0.7 dynamic_slice.117
  76.0 1.3 convert_reduce_fusion.3
  78.9 1.0 collective-permute-start.1
  80.0 5.3 %collective-permute-done.1 = f32[128,512]{0,1:T(8,128)S(1)} collective-permute-done((f32[128,512]{0,1:T(8,128)S(1)}, f32[128,512]{0,1:T(8,128)S(1)}, u32[]{:S(2)}, u32[]{:S(2)}) %collective-permute-start.1) | collective-permute-done | bytes 262176 | tf_op jit(solution)/shard_map/while/body/eval_jaxpr/ppermute | solution.py:12
  85.5 0.7 dynamic_slice.117
  86.1 1.3 convert_reduce_fusion.3
  87.4 0.6 fusion.81
  88.4 6.2 %while.88 = (s32[]{:T(128)}, f32[128,512]{0,1:T(8,128)S(1)}, f32[1024,256]{0,1:T(8,128)S(1)}, s32[]{:T(128)}, s32[2]{0:T(128)S(1)}, /*index=5*/bf16[1024,256]{1,...) while((s32[]{:T(128)}, f32[128,512]{0,1:T(8,128)S(1)}, ...), condition=%wide.region_6.6_spmd.clone, body=%wide.region_5.5_spmd.clone.sunk | while | flops 84574488 | bytes 3415011 | solution.py:114
  94.7 1.0 collective-permute-start.1
  95.7 4.8 %collective-permute-done.1 = f32[128,512]{0,1:T(8,128)S(1)} collective-permute-done((f32[128,512]{0,1:T(8,128)S(1)}, f32[128,512]{0,1:T(8,128)S(1)}, u32[]{:S(2)}, u32[]{:S(2)}) %collective-permute-start.1) | collective-permute-done | bytes 262176 | tf_op jit(solution)/shard_map/while/body/eval_jaxpr/ppermute | solution.py:12
  100.9 6.4 %while.87 = (s32[]{:T(128)}, f32[128,512]{0,1:T(8,128)S(1)}, f32[1024,256]{0,1:T(8,128)S(1)}, s32[]{:T(128)}, s32[2]{0:T(128)S(1)}, /*index=5*/bf16[1024,256]{1,...) while((s32[]{:T(128)}, f32[128,512]{0,1:T(8,128)S(1)}, ...), condition=%wide.region_13.14_spmd.clone.clone, body=%wide.region_12.13_spmd.clone.clone.sunk | while | flops 84574488 | bytes 3414491 | solution.py:114
  107.4 1.3 copy.67
  108.9 5.8 %collective-permute-done.3 = f32[128,512]{1,0:T(8,128)S(1)} collective-permute-done((f32[128,512]{1,0:T(8,128)S(1)}, f32[128,512]{1,0:T(8,128)S(1)}, u32[]{:S(2)}, u32[]{:S(2)}) %collective-permute-start.3) | collective-permute-done | bytes 262176 | tf_op jit(solution)/shard_map/ppermute | solution.py:12
  114.7 59.6 %reduce-scatter.2.cloned.1.call-done = f32[128,256]{1,0:T(8,128)} async-done(((f32[1024,256]{1,0:T(8,128)}), f32[128,256]{1,0:T(8,128)}) %reduce-scatter.2.cloned.1.call-update) | async-done | bytes 131088 | tf_op jit(solution)/shard_map/reduce_scatter | solution.py:137
  174.3 1.5 fusion.43
  175.8 0.7 copy.125
  (105 shorter events, 12.1 us)
Async XLA Ops:
  7.2 167.1 %reduce-scatter.2.cloned.1.call-start = ((), (), s32[]{:S(2)}) async-start(), calls=%async_computation.1 | async-start | bytes 1179648 | tf_op jit(solution)/shard_map/reduce_scatter | solution.py:137
  7.9 0.7 copy-start.6
  16.4 0.7 copy-start.5
  24.5 1.1 copy-start.1
  25.6 0.9 copy-start.2
  26.5 0.8 copy-start.3
  26.5 0.8 copy-start.4
  59.3 0.7 copy-start
  60.0 15.2 %collective-permute-start = (bf16[3,128,512]{1,2,0:T(8,128)(2,1)S(1)}, bf16[3,128,512]{1,2,0:T(8,128)(2,1)S(1)}, u32[]{:S(2)}, u32[]{:S(2)}) collective-permute-start(bf16[3,128,512]{1,2,0:T(8,128)(2,1)S(1)} %copy.101), channel_id=1, source_target_pairs={{0,1},{1,2},{2,3},{3,0},{4,5},{5,6},{6,7},{7,4},{8,9},{9,10},{10,1... | collective-permute-start | bytes 1179656 | tf_op jit(solution)/shard_map/while/body/eval_jaxpr/ppermute | solution.py:12
  69.3 5.8 %collective-permute-start.1 = (f32[128,512]{0,1:T(8,128)S(1)}, f32[128,512]{0,1:T(8,128)S(1)}, u32[]{:S(2)}, u32[]{:S(2)}) collective-permute-start(f32[128,512]{0,1:T(8,128)S(1)} %get-tuple-element.1444), channel_id=1, source_target_pairs={{0,1},{1,2},{2,3},{3,0},{4,5},{5,6},{6,7},{7,4},{8,9},{9,10},{10,1... | collective-permute-start | bytes 786440 | tf_op jit(solution)/shard_map/while/body/eval_jaxpr/ppermute | solution.py:12
  70.3 4.9 %collective-permute-start.2 = (f32[1,4,128]{2,1,0:T(4,128)S(1)}, f32[1,4,128]{2,1,0:T(4,128)S(1)}, u32[]{:S(2)}, u32[]{:S(2)}) collective-permute-start(f32[1,4,128]{2,1,0:T(4,128)S(1)} %get-tuple-element.1678), channel_id=1, source_target_pairs={{0,1},{1,2},{2,3},{3,0},{4,5},{5,6},{6,7},{7,4},{8,9},{9,10},{10,1... | collective-permute-start | bytes 6152 | tf_op jit(solution)/shard_map/while/body/eval_jaxpr/ppermute | solution.py:12
  75.2 10.1 %collective-permute-start = (bf16[3,128,512]{1,2,0:T(8,128)(2,1)S(1)}, bf16[3,128,512]{1,2,0:T(8,128)(2,1)S(1)}, u32[]{:S(2)}, u32[]{:S(2)}) collective-permute-start(bf16[3,128,512]{1,2,0:T(8,128)(2,1)S(1)} %copy.101), channel_id=1, source_target_pairs={{0,1},{1,2},{2,3},{3,0},{4,5},{5,6},{6,7},{7,4},{8,9},{9,10},{10,1... | collective-permute-start | bytes 1179656 | tf_op jit(solution)/shard_map/while/body/eval_jaxpr/ppermute | solution.py:12
  78.9 6.3 %collective-permute-start.1 = (f32[128,512]{0,1:T(8,128)S(1)}, f32[128,512]{0,1:T(8,128)S(1)}, u32[]{:S(2)}, u32[]{:S(2)}) collective-permute-start(f32[128,512]{0,1:T(8,128)S(1)} %get-tuple-element.1444), channel_id=1, source_target_pairs={{0,1},{1,2},{2,3},{3,0},{4,5},{5,6},{6,7},{7,4},{8,9},{9,10},{10,1... | collective-permute-start | bytes 786440 | tf_op jit(solution)/shard_map/while/body/eval_jaxpr/ppermute | solution.py:12
  79.9 5.4 %collective-permute-start.2 = (f32[1,4,128]{2,1,0:T(4,128)S(1)}, f32[1,4,128]{2,1,0:T(4,128)S(1)}, u32[]{:S(2)}, u32[]{:S(2)}) collective-permute-start(f32[1,4,128]{2,1,0:T(4,128)S(1)} %get-tuple-element.1678), channel_id=1, source_target_pairs={{0,1},{1,2},{2,3},{3,0},{4,5},{5,6},{6,7},{7,4},{8,9},{9,10},{10,1... | collective-permute-start | bytes 6152 | tf_op jit(solution)/shard_map/while/body/eval_jaxpr/ppermute | solution.py:12
  85.4 15.2 %collective-permute-start = (bf16[3,128,512]{1,2,0:T(8,128)(2,1)S(1)}, bf16[3,128,512]{1,2,0:T(8,128)(2,1)S(1)}, u32[]{:S(2)}, u32[]{:S(2)}) collective-permute-start(bf16[3,128,512]{1,2,0:T(8,128)(2,1)S(1)} %copy.101), channel_id=1, source_target_pairs={{0,1},{1,2},{2,3},{3,0},{4,5},{5,6},{6,7},{7,4},{8,9},{9,10},{10,1... | collective-permute-start | bytes 1179656 | tf_op jit(solution)/shard_map/while/body/eval_jaxpr/ppermute | solution.py:12
  94.7 5.8 %collective-permute-start.1 = (f32[128,512]{0,1:T(8,128)S(1)}, f32[128,512]{0,1:T(8,128)S(1)}, u32[]{:S(2)}, u32[]{:S(2)}) collective-permute-start(f32[128,512]{0,1:T(8,128)S(1)} %get-tuple-element.1444), channel_id=1, source_target_pairs={{0,1},{1,2},{2,3},{3,0},{4,5},{5,6},{6,7},{7,4},{8,9},{9,10},{10,1... | collective-permute-start | bytes 786440 | tf_op jit(solution)/shard_map/while/body/eval_jaxpr/ppermute | solution.py:12
  95.6 4.9 %collective-permute-start.2 = (f32[1,4,128]{2,1,0:T(4,128)S(1)}, f32[1,4,128]{2,1,0:T(4,128)S(1)}, u32[]{:S(2)}, u32[]{:S(2)}) collective-permute-start(f32[1,4,128]{2,1,0:T(4,128)S(1)} %get-tuple-element.1678), channel_id=1, source_target_pairs={{0,1},{1,2},{2,3},{3,0},{4,5},{5,6},{6,7},{7,4},{8,9},{9,10},{10,1... | collective-permute-start | bytes 6152 | tf_op jit(solution)/shard_map/while/body/eval_jaxpr/ppermute | solution.py:12
  108.9 5.8 %collective-permute-start.3 = (f32[128,512]{1,0:T(8,128)S(1)}, f32[128,512]{1,0:T(8,128)S(1)}, u32[]{:S(2)}, u32[]{:S(2)}) collective-permute-start(f32[128,512]{1,0:T(8,128)S(1)} %copy.66), channel_id=1, source_target_pairs={{0,1},{1,2},{2,3},{3,0},{4,5},{5,6},{6,7},{7,4},{8,9},{9,10},{10,1... | collective-permute-start | bytes 786440 | tf_op jit(solution)/shard_map/ppermute | solution.py:12
Sparse Core Ops, SparseCore 0:
  108.9 65.3 reduce-scatter.1
where the time goes:
time: 184 us; the launch traced here: 183 us
  waiting for transfers between devices  80.3 us (44%)
  blocking collectives  43.3 us (24%)
  between operations  14.8 us (8%)
  loops' own time  14.6 us (8%)
  local copies, waits for them, and re-layouts  14.4 us (8%)
  other arithmetic  9.58 us (5%)
  starting transfers between devices  3.4 us (2%)
  matrix products  2.9 us (2%)
    reduce_scatter x1, waiting for transfers between devices, shards(): lax.psum_scatter(key_grads, 'pb', scatter_dimension=0, tiled=True)  59.6 us
    all_gather x1, blocking collectives, shards(): column_keys = lax.all_gather(key_pairs, 'pb', axis=0, tiled=True)  31.9 us
    ppermute x10, waiting for transfers between devices, passed_along(): return lax.ppermute(value, axis, pairs)  20.7 us
    another operation x4, loops' own time, visit_block(): return lax.fori_loop(0, live_tiles, one_tile, (query_grad, key_grads))  14.3 us
    unnamed x21, local copies, waits for them, and re-layouts  6.74 us
    unnamed x1, blocking collectives  6.38 us
    reduce_sum x4, other arithmetic, visit_block(): live_tiles = jnp.sum(wanted.astype(jnp.int32))  5.18 us
    all_gather x1, blocking collectives, shards(): lax.all_gather(selected, 'ka', axis=0, tiled=True)  5.05 us
  transfers between devices with their start and end apart: 11, of which 5 were waited for; matrix products, arithmetic and copies ran while one was open for 7% of the time, Pallas kernels for 0%

commit v1 on v0

--- a/solution.py
+++ b/solution.py
@@ -29,7 +29,9 @@
     block_rows = query_rows.shape[0] // block_count
     score_scale = head_width ** (-0.5)
     key_pairs = jnp.concatenate([key_rows, value_rows], 1)
-    column_keys = lax.all_gather(key_pairs, "pb", axis=0, tiled=True)
+    column_keys = jnp.concatenate(
+        lax.all_to_all(jnp.stack([key_pairs] * lax.axis_size("pb")), "pb", 0, 0), axis=0
+    )
     peer_slots, peer_counts = (
         lax.all_gather(selected, "ka", axis=0, tiled=True),
         lax.all_gather(counts, "ka", axis=0, tiled=True),

time: 184 us -> 162 us (0.88)
  blocking collectives: 43.3 us -> 9.95 us
  starting transfers between devices: 3.4 us -> 10.8 us
  waiting for transfers between devices: 80.3 us -> 83.2 us
    all_gather x1 -> x0, blocking collectives: 31.9 us -> none  [shards(): column_keys = lax.all_gather(key_pairs, 'pb', axis=0, tiled=True)]
    all_to_all x0 -> x1, starting transfers between devices: none -> 7.44 us  [shards(): lax.all_to_all(jnp.stack([key_pairs] * lax.axis_size('pb')), 'pb', 0, 0)]
    reduce_scatter x1, waiting for transfers between devices: 59.6 us -> 62.3 us  [shards(): lax.psum_scatter(key_grads, 'pb', scatter_dimension=0, tiled=True)]
    unnamed x21 -> x19, local copies, waits for them, and re-layouts: 6.74 us -> 5.82 us
  transfers between devices with their start and end apart: 11 -> 12, of which waited for: 5 -> 5; matrix products, arithmetic and copies ran while one was open for 7% -> 10% of each run, Pallas kernels for 0% -> 0%
where the time goes in v1:
time: 162 us; the launch traced here: 161 us
  waiting for transfers between devices  83.2 us (51%)
  loops' own time  14.8 us (9%)
  between operations  14.8 us (9%)
  local copies, waits for them, and re-layouts  14.2 us (9%)
  starting transfers between devices  10.8 us (7%)
  other arithmetic  10.1 us (6%)
  blocking collectives  9.95 us (6%)
  matrix products  2.91 us (2%)
    reduce_scatter x1, waiting for transfers between devices, shards(): lax.psum_scatter(key_grads, 'pb', scatter_dimension=0, tiled=True)  62.3 us
    ppermute x10, waiting for transfers between devices, passed_along(): return lax.ppermute(value, axis, pairs)  20.8 us
    another operation x4, loops' own time, visit_block(): return lax.fori_loop(0, live_tiles, one_tile, (query_grad, key_grads))  14.5 us
    all_to_all x1, starting transfers between devices, shards(): lax.all_to_all(jnp.stack([key_pairs] * lax.axis_size('pb')), 'pb', 0, 0)  7.44 us
    unnamed x19, local copies, waits for them, and re-layouts  5.82 us
    reduce_sum x4, other arithmetic, visit_block(): live_tiles = jnp.sum(wanted.astype(jnp.int32))  5.08 us
    all_gather x1, blocking collectives, shards(): lax.all_gather(selected, 'ka', axis=0, tiled=True)  5.05 us
    unnamed x1, blocking collectives  4.9 us
  transfers between devices with their start and end apart: 12, of which 5 were waited for; matrix products, arithmetic and copies ran while one was open for 10% of the time, Pallas kernels for 0%

profile of v1, /device:TPU:0, one launch (start us, length us, event | category | flops | bytes accessed | tf_op | source)
XLA Modules:
  0.0 160.8 jit_solution(6251212711825602742)
XLA Ops:
  7.2 0.8 pad_maximum_fusion.1
  7.9 0.8 stack.27
  8.8 7.4 %all-to-all-start = ((bf16[8,128,256]{2,1,0:T(8,128)(2,1)}), bf16[8,128,256]{2,1,0:T(8,128)(2,1)S(1)}, u32[]{:S(2)}, u32[]{:S(2)}) async-start(bf16[8,128,256]{2,1,0:T(8,128)(2,1)} %stack.27), calls=%async_computation | async-start | bytes 1048576 | tf_op jit(solution)/shard_map/all_to_all | solution.py:33
  16.9 0.6 copy-done.5
  18.2 0.8 dynamic-update-slice
  18.9 0.7 copy-done.4
  19.6 5.0 %all-gather = s32[4,1,2]{2,1,0:T(1,128)S(1)} all-gather(s32[1,1,2]{2,1,0:T(1,128)S(1)} %bitcast.224), channel_id=1, replica_groups=mesh['pb'=8,'ka'=4] {'ka'}, dimensions={0}, use_global_device_ids=true | all-gather | bytes 40 | tf_op jit(solution)/shard_map/all_gather | solution.py:36
  24.6 4.9 %all-reduce = s32[4]{0:T(128)S(1)} all-reduce(s32[4]{0:T(128)S(1)} %dynamic-update-slice), channel_id=1, replica_groups=mesh['pb'=8,'ka'=4] {'ka'}, use_global_device_ids=true, to_apply=%add | all-reduce | flops 4 | bytes 32
  29.6 0.8 copy-done.2
  30.5 0.8 copy-done.3
  32.9 1.2 convert_reduce_fusion.1
  35.0 40.7 %while.86 = (s32[]{:T(128)}, bf16[3,128,512]{1,2,0:T(8,128)(2,1)S(1)}, f32[128,512]{0,1:T(8,128)S(1)}, f32[1,4,128]{2,1,0:T(4,128)S(1)}, f32[1024,256]{0,1:T(8,1...) while((s32[]{:T(128)}, ...), condition=%wide.region_7.8_spmd.clone.clone, body=%wide.region_0.7_spmd.clone.clone.sunk | while | flops 84836216 | bytes 8673559 | solution.py:132
  35.7 1.3 convert_reduce_fusion.3
  37.9 6.4 %while.88 = (s32[]{:T(128)}, f32[128,512]{0,1:T(8,128)S(1)}, f32[1024,256]{0,1:T(8,128)S(1)}, s32[]{:T(128)}, s32[2]{0:T(128)S(1)}, /*index=5*/bf16[1024,256]{1,...) while((s32[]{:T(128)}, f32[128,512]{0,1:T(8,128)S(1)}, ...), condition=%wide.region_6.6_spmd.clone, body=%wide.region_5.5_spmd.clone.sunk | while | flops 84574488 | bytes 3415011 | solution.py:116
  38.6 0.7 dynamic_slice.121
  44.4 1.0 collective-permute-start.1
  45.4 4.8 %collective-permute-done.1 = f32[128,512]{0,1:T(8,128)S(1)} collective-permute-done((f32[128,512]{0,1:T(8,128)S(1)}, f32[128,512]{0,1:T(8,128)S(1)}, u32[]{:S(2)}, u32[]{:S(2)}) %collective-permute-start.1) | collective-permute-done | bytes 262176 | tf_op jit(solution)/shard_map/while/body/eval_jaxpr/ppermute | solution.py:12
  51.0 1.3 convert_reduce_fusion.3
  53.2 0.7 while.88
  53.9 1.0 collective-permute-start.1
  55.0 5.4 %collective-permute-done.1 = f32[128,512]{0,1:T(8,128)S(1)} collective-permute-done((f32[128,512]{0,1:T(8,128)S(1)}, f32[128,512]{0,1:T(8,128)S(1)}, u32[]{:S(2)}, u32[]{:S(2)}) %collective-permute-start.1) | collective-permute-done | bytes 262176 | tf_op jit(solution)/shard_map/while/body/eval_jaxpr/ppermute | solution.py:12
  61.1 1.3 convert_reduce_fusion.3
  63.4 6.4 %while.88 = (s32[]{:T(128)}, f32[128,512]{0,1:T(8,128)S(1)}, f32[1024,256]{0,1:T(8,128)S(1)}, s32[]{:T(128)}, s32[2]{0:T(128)S(1)}, /*index=5*/bf16[1024,256]{1,...) while((s32[]{:T(128)}, f32[128,512]{0,1:T(8,128)S(1)}, ...), condition=%wide.region_6.6_spmd.clone, body=%wide.region_5.5_spmd.clone.sunk | while | flops 84574488 | bytes 3415011 | solution.py:116
  64.1 0.7 dynamic_slice.121
  69.8 1.0 collective-permute-start.1
  70.9 4.8 %collective-permute-done.1 = f32[128,512]{0,1:T(8,128)S(1)} collective-permute-done((f32[128,512]{0,1:T(8,128)S(1)}, f32[128,512]{0,1:T(8,128)S(1)}, u32[]{:S(2)}, u32[]{:S(2)}) %collective-permute-start.1) | collective-permute-done | bytes 262176 | tf_op jit(solution)/shard_map/while/body/eval_jaxpr/ppermute | solution.py:12
  75.8 6.2 %while.87 = (s32[]{:T(128)}, f32[128,512]{0,1:T(8,128)S(1)}, f32[1024,256]{0,1:T(8,128)S(1)}, s32[]{:T(128)}, s32[2]{0:T(128)S(1)}, /*index=5*/bf16[1024,256]{1,...) while((s32[]{:T(128)}, f32[128,512]{0,1:T(8,128)S(1)}, ...), condition=%wide.region_13.14_spmd.clone.clone, body=%wide.region_12.13_spmd.clone.clone.sunk | while | flops 84574488 | bytes 3414491 | solution.py:116
  82.0 1.3 copy.67
  83.6 5.8 %collective-permute-done.3 = f32[128,512]{1,0:T(8,128)S(1)} collective-permute-done((f32[128,512]{1,0:T(8,128)S(1)}, f32[128,512]{1,0:T(8,128)S(1)}, u32[]{:S(2)}, u32[]{:S(2)}) %collective-permute-start.3) | collective-permute-done | bytes 262176 | tf_op jit(solution)/shard_map/ppermute | solution.py:12
  89.4 62.3 %reduce-scatter.2.cloned.1.call-done = f32[128,256]{1,0:T(8,128)} async-done(((f32[1024,256]{1,0:T(8,128)}), f32[128,256]{1,0:T(8,128)}) %reduce-scatter.2.cloned.1.call-update) | async-done | bytes 131088 | tf_op jit(solution)/shard_map/reduce_scatter | solution.py:139
  151.7 1.5 fusion.43
  153.2 0.7 copy.125
  (105 shorter events, 12.6 us)
Async XLA Ops:
  8.8 20.7 %copy-start.1 = (bf16[128,512]{1,0:T(8,128)(2,1)S(1)}, bf16[128,512]{1,0:T(8,128)(2,1)}, u32[]{:S(2)}) copy-start(bf16[128,512]{1,0:T(8,128)(2,1)} %param.17) | copy-start | bytes 393220
  8.8 25.5 %all-to-all-start = ((bf16[8,128,256]{2,1,0:T(8,128)(2,1)}), bf16[8,128,256]{2,1,0:T(8,128)(2,1)S(1)}, u32[]{:S(2)}, u32[]{:S(2)}) async-start(bf16[8,128,256]{2,1,0:T(8,128)(2,1)} %stack.27), calls=%async_computation | async-start | bytes 1048576 | tf_op jit(solution)/shard_map/all_to_all | solution.py:33
  16.2 135.5 %reduce-scatter.2.cloned.1.call-start = ((), (), s32[]{:S(2)}) async-start(), calls=%async_computation.2 | async-start | bytes 1179648 | tf_op jit(solution)/shard_map/reduce_scatter | solution.py:139
  16.9 0.7 copy-start.5
  18.9 0.7 copy-start.4
  29.5 0.9 copy-start.2
  30.4 0.9 copy-start.3
  34.3 0.7 copy-start
  35.0 15.2 %collective-permute-start = (bf16[3,128,512]{1,2,0:T(8,128)(2,1)S(1)}, bf16[3,128,512]{1,2,0:T(8,128)(2,1)S(1)}, u32[]{:S(2)}, u32[]{:S(2)}) collective-permute-start(bf16[3,128,512]{1,2,0:T(8,128)(2,1)S(1)} %copy.101), channel_id=1, source_target_pairs={{0,1},{1,2},{2,3},{3,0},{4,5},{5,6},{6,7},{7,4},{8,9},{9,10},{10,1... | collective-permute-start | bytes 1179656 | tf_op jit(solution)/shard_map/while/body/eval_jaxpr/ppermute | solution.py:12
  44.4 5.8 %collective-permute-start.1 = (f32[128,512]{0,1:T(8,128)S(1)}, f32[128,512]{0,1:T(8,128)S(1)}, u32[]{:S(2)}, u32[]{:S(2)}) collective-permute-start(f32[128,512]{0,1:T(8,128)S(1)} %get-tuple-element.1444), channel_id=1, source_target_pairs={{0,1},{1,2},{2,3},{3,0},{4,5},{5,6},{6,7},{7,4},{8,9},{9,10},{10,1... | collective-permute-start | bytes 786440 | tf_op jit(solution)/shard_map/while/body/eval_jaxpr/ppermute | solution.py:12
  45.4 4.9 %collective-permute-start.2 = (f32[1,4,128]{2,1,0:T(4,128)S(1)}, f32[1,4,128]{2,1,0:T(4,128)S(1)}, u32[]{:S(2)}, u32[]{:S(2)}) collective-permute-start(f32[1,4,128]{2,1,0:T(4,128)S(1)} %get-tuple-element.1679), channel_id=1, source_target_pairs={{0,1},{1,2},{2,3},{3,0},{4,5},{5,6},{6,7},{7,4},{8,9},{9,10},{10,1... | collective-permute-start | bytes 6152 | tf_op jit(solution)/shard_map/while/body/eval_jaxpr/ppermute | solution.py:12
  50.3 10.1 %collective-permute-start = (bf16[3,128,512]{1,2,0:T(8,128)(2,1)S(1)}, bf16[3,128,512]{1,2,0:T(8,128)(2,1)S(1)}, u32[]{:S(2)}, u32[]{:S(2)}) collective-permute-start(bf16[3,128,512]{1,2,0:T(8,128)(2,1)S(1)} %copy.101), channel_id=1, source_target_pairs={{0,1},{1,2},{2,3},{3,0},{4,5},{5,6},{6,7},{7,4},{8,9},{9,10},{10,1... | collective-permute-start | bytes 1179656 | tf_op jit(solution)/shard_map/while/body/eval_jaxpr/ppermute | solution.py:12
  53.9 6.5 %collective-permute-start.1 = (f32[128,512]{0,1:T(8,128)S(1)}, f32[128,512]{0,1:T(8,128)S(1)}, u32[]{:S(2)}, u32[]{:S(2)}) collective-permute-start(f32[128,512]{0,1:T(8,128)S(1)} %get-tuple-element.1444), channel_id=1, source_target_pairs={{0,1},{1,2},{2,3},{3,0},{4,5},{5,6},{6,7},{7,4},{8,9},{9,10},{10,1... | collective-permute-start | bytes 786440 | tf_op jit(solution)/shard_map/while/body/eval_jaxpr/ppermute | solution.py:12
  54.9 5.5 %collective-permute-start.2 = (f32[1,4,128]{2,1,0:T(4,128)S(1)}, f32[1,4,128]{2,1,0:T(4,128)S(1)}, u32[]{:S(2)}, u32[]{:S(2)}) collective-permute-start(f32[1,4,128]{2,1,0:T(4,128)S(1)} %get-tuple-element.1679), channel_id=1, source_target_pairs={{0,1},{1,2},{2,3},{3,0},{4,5},{5,6},{6,7},{7,4},{8,9},{9,10},{10,1... | collective-permute-start | bytes 6152 | tf_op jit(solution)/shard_map/while/body/eval_jaxpr/ppermute | solution.py:12
  60.5 15.2 %collective-permute-start = (bf16[3,128,512]{1,2,0:T(8,128)(2,1)S(1)}, bf16[3,128,512]{1,2,0:T(8,128)(2,1)S(1)}, u32[]{:S(2)}, u32[]{:S(2)}) collective-permute-start(bf16[3,128,512]{1,2,0:T(8,128)(2,1)S(1)} %copy.101), channel_id=1, source_target_pairs={{0,1},{1,2},{2,3},{3,0},{4,5},{5,6},{6,7},{7,4},{8,9},{9,10},{10,1... | collective-permute-start | bytes 1179656 | tf_op jit(solution)/shard_map/while/body/eval_jaxpr/ppermute | solution.py:12
  69.8 5.8 %collective-permute-start.1 = (f32[128,512]{0,1:T(8,128)S(1)}, f32[128,512]{0,1:T(8,128)S(1)}, u32[]{:S(2)}, u32[]{:S(2)}) collective-permute-start(f32[128,512]{0,1:T(8,128)S(1)} %get-tuple-element.1444), channel_id=1, source_target_pairs={{0,1},{1,2},{2,3},{3,0},{4,5},{5,6},{6,7},{7,4},{8,9},{9,10},{10,1... | collective-permute-start | bytes 786440 | tf_op jit(solution)/shard_map/while/body/eval_jaxpr/ppermute | solution.py:12
  70.8 4.9 %collective-permute-start.2 = (f32[1,4,128]{2,1,0:T(4,128)S(1)}, f32[1,4,128]{2,1,0:T(4,128)S(1)}, u32[]{:S(2)}, u32[]{:S(2)}) collective-permute-start(f32[1,4,128]{2,1,0:T(4,128)S(1)} %get-tuple-element.1679), channel_id=1, source_target_pairs={{0,1},{1,2},{2,3},{3,0},{4,5},{5,6},{6,7},{7,4},{8,9},{9,10},{10,1... | collective-permute-start | bytes 6152 | tf_op jit(solution)/shard_map/while/body/eval_jaxpr/ppermute | solution.py:12
  83.5 5.8 %collective-permute-start.3 = (f32[128,512]{1,0:T(8,128)S(1)}, f32[128,512]{1,0:T(8,128)S(1)}, u32[]{:S(2)}, u32[]{:S(2)}) collective-permute-start(f32[128,512]{1,0:T(8,128)S(1)} %copy.66), channel_id=1, source_target_pairs={{0,1},{1,2},{2,3},{3,0},{4,5},{5,6},{6,7},{7,4},{8,9},{9,10},{10,1... | collective-permute-start | bytes 786440 | tf_op jit(solution)/shard_map/ppermute | solution.py:12
Sparse Core Ops, SparseCore 0:
  83.5 68.1 reduce-scatter.1
